TPU v7x, 32 devices: a whole 2x2x4 slice. The times are simulated.
32 devices in a mesh: grp: 4 (over z), shard: 8 (over y, x, core).
Axes of the slice: x: 2, y: 2, z: 4, core: 2. Of those that a mesh axis runs over, the one named last changes fastest.
Arguments:
- latents: bfloat16 [4096, 1024], P(('grp', 'shard')), may hold values from -6 to 6
- head_weight: bfloat16 [1024, 1024], P('shard'), may hold values from -0.1875 to 0.1875
- norm_gain: float32 [1024], replicated, may hold values from 0.1 to 1.9
- color_head: bfloat16 [4, 256], replicated, may hold values from -1.5 to 1.5
- sample_points: float32 [2048, 192], P(('grp', 'shard')), may hold values from -1 to 1
- sample_spacing: float32 [2048, 64], P(('grp', 'shard')), may hold values from 0.002 to 0.02
- ray_targets: float32 [3, 2048], P(None, ('grp', 'shard')), may hold values from 0 to 1
- ray_scene: int32 [2048], P(('grp', 'shard')), may hold values from 0 to 31, as said below
Outputs:
- rendered_color: float32 [3, 2048], P(None, ('grp', 'shard'))
- loss: float32 [], replicated
- head_grad: float32 [1024, 1024], P('shard')
- norm_gain_grad: float32 [1024], replicated
- latent_grad: bfloat16 [4096, 1024], P(('grp', 'shard'))
Inputs may be any that keep to these rules, and one draw needn't show every extreme that they name: `ray_scene`: one scene, drawn from the seed, is named by exactly 8 rays of every device; no device names any scene more than 8 times; every scene is named by one ray or more, and the totals of the other scenes differ from one another by one at most.
All inputs are finite; a program needn't handle non-finite values.
Results may differ from a plain program's by a relative error of at most 0.017.
Values may be sent and summed in bfloat16 or wider, within the bound.
A program may use at most 64 MiB of HBM per device.

v0:
```python
import math
import jax
import jax.numpy as jnp
from jax import lax
from jax.sharding import PartitionSpec as P

norm_eps = 1e-06


def encode(sample_rows, field_width):
    column = jnp.arange(field_width)
    component = column % 3
    octave = (column // 6 % 8).astype(jnp.float32)
    frequency = jnp.exp2(octave) * math.pi
    phase_shift = (column // 3 % 2).astype(jnp.float32) * (0.5 * math.pi)
    picked = jnp.zeros((sample_rows.shape[0], field_width), jnp.float32)
    for coord in range(3):
        chosen = (component == coord).astype(jnp.float32)
        picked = picked + sample_rows[:, coord : coord + 1] * chosen[None, :]
    return jnp.sin(picked * frequency + phase_shift)


def point_rows(points, ray_depth):
    ray_number = points.shape[0]
    return (
        points.reshape(ray_number, 3, ray_depth)
        .transpose(0, 2, 1)
        .reshape(ray_number * ray_depth, 3)
    )


def render_rays(points, spacing, target, live_rays, scene_factor, w_first, w_second, color_head):
    ray_number, ray_depth = spacing.shape
    field_width = w_first.shape[0]
    fan_scale = field_width ** (-0.5)
    sample_rows = point_rows(points, ray_depth)
    h_zero = encode(sample_rows, field_width).astype(jnp.bfloat16)
    h_one = jax.nn.relu(
        jnp.dot(h_zero, w_first, preferred_element_type=jnp.float32) * fan_scale
    ).astype(jnp.bfloat16)
    h_two = jax.nn.relu(
        jnp.dot(h_one, w_second, preferred_element_type=jnp.float32) * fan_scale
    ).astype(jnp.bfloat16)
    raw_out = lax.dot_general(
        color_head, h_two, (((1,), (1,)), ((), ())), preferred_element_type=jnp.float32
    )
    density = jax.nn.softplus(raw_out[0]).reshape(ray_number, ray_depth)
    albedo = jax.nn.sigmoid(raw_out[1:4]).reshape(3, ray_number, ray_depth)
    optical = density * spacing
    optical_before = jnp.cumsum(optical, axis=1) - optical
    transmit = jnp.exp(-optical_before)
    survive = jnp.exp(-optical)
    blend = transmit * (1.0 - survive)
    ray_color = jnp.sum(blend[None] * (albedo - 1.0), axis=2) + 1.0
    residual = ray_color - target.T
    loss_part = jnp.sum(
        jnp.where(live_rays, jnp.sum(residual * residual, axis=0) * scene_factor, 0.0)
    )
    grad_color = jnp.where(live_rays[None, :], 2.0 * residual * scene_factor, 0.0)
    d_albedo = grad_color[:, :, None] * blend[None]
    d_blend = jnp.sum(grad_color[:, :, None] * (albedo - 1.0), axis=0)
    weighted = d_blend * blend
    behind = jnp.sum(weighted, axis=1, keepdims=True) - jnp.cumsum(weighted, axis=1)
    d_optical = d_blend * transmit * survive - behind
    d_density = (
        d_optical * spacing * jax.nn.sigmoid(raw_out[0]).reshape(ray_number, ray_depth)
    ).reshape(1, ray_number * ray_depth)
    d_tint = (d_albedo * albedo * (1.0 - albedo)).reshape(3, ray_number * ray_depth)
    d_raw = jnp.concatenate([d_density, d_tint], axis=0).astype(jnp.bfloat16)
    d_htwo = lax.dot_general(
        d_raw, color_head, (((0,), (0,)), ((), ())), preferred_element_type=jnp.float32
    )
    d_atwo = (jnp.where(h_two > 0, d_htwo, 0.0) * fan_scale).astype(jnp.bfloat16)
    grad_second = lax.dot_general(
        h_one, d_atwo, (((0,), (0,)), ((), ())), preferred_element_type=jnp.float32
    )
    d_hone = lax.dot_general(
        d_atwo, w_second, (((1,), (1,)), ((), ())), preferred_element_type=jnp.float32
    )
    d_aone = (jnp.where(h_one > 0, d_hone, 0.0) * fan_scale).astype(jnp.bfloat16)
    grad_first = lax.dot_general(
        h_zero, d_aone, (((0,), (0,)), ((), ())), preferred_element_type=jnp.float32
    )
    return (ray_color, loss_part, grad_first, grad_second)


def body(
    latents,
    head_weight,
    norm_gain,
    color_head,
    sample_points,
    sample_spacing,
    ray_targets,
    ray_scene,
):
    devices = lax.axis_size(("grp", "shard"))
    ray_count, ray_depth = sample_spacing.shape
    tokens, model = latents.shape
    field_width = color_head.shape[1]
    per_layer = field_width * field_width // model
    per_device = 4 * ray_count // devices
    slot_total = per_device * devices
    latent_f32 = latents.astype(jnp.float32)
    inv_rms = lax.rsqrt(jnp.mean(latent_f32 * latent_f32, axis=1, keepdims=True) + norm_eps)
    x_hat = latent_f32 * inv_rms
    x_norm = (x_hat * norm_gain).astype(jnp.bfloat16)
    columns = x_norm
    field_sum = jnp.dot(
        columns,
        lax.all_gather(head_weight, "shard", axis=0, tiled=True),
        preferred_element_type=jnp.float32,
    )
    field_rows = field_sum.astype(jnp.bfloat16)
    w_first = field_rows[:per_layer].reshape(field_width, field_width)
    w_second = field_rows[per_layer:].reshape(field_width, field_width)
    ray_ids = jnp.arange(ray_count, dtype=jnp.int32)
    same_scene = ray_scene[:, None] == ray_scene[None, :]
    earlier = ray_ids[:, None] < ray_ids[None, :]
    ray_rank = jnp.sum(jnp.logical_and(same_scene, earlier).astype(jnp.int32), axis=0)
    slot_of_ray = ray_scene * per_device + ray_rank
    payload = jnp.concatenate([sample_points, sample_spacing], axis=1)
    send_payload = (
        jnp.zeros((slot_total, payload.shape[1]), jnp.float32).at[slot_of_ray].set(payload)
    )
    send_target = jnp.zeros((slot_total, 3), jnp.float32).at[slot_of_ray].set(ray_targets.T)
    send_live = jnp.zeros((slot_total,), jnp.float32).at[slot_of_ray].set(1.0)
    recv_payload, recv_target, recv_live = (
        lax.all_to_all(send_payload, ("grp", "shard"), split_axis=0, concat_axis=0, tiled=True),
        lax.all_to_all(send_target, ("grp", "shard"), split_axis=0, concat_axis=0, tiled=True),
        lax.all_to_all(send_live, ("grp", "shard"), split_axis=0, concat_axis=0, tiled=True),
    )
    block_rays = 1024 // ray_depth
    block_total = slot_total // block_rays
    scene_rays = jnp.sum(recv_live)
    scene_factor = 1.0 / (devices * scene_rays)

    def render_block(running, block_item):
        grad_first, grad_second, loss_sum = running
        block_payload, block_target, block_live = block_item
        ray_color, loss_part, more_first, more_second = render_rays(
            block_payload[:, : 3 * ray_depth],
            block_payload[:, 3 * ray_depth :],
            block_target,
            block_live > 0.5,
            scene_factor,
            w_first,
            w_second,
            color_head,
        )
        return (
            (grad_first + more_first, grad_second + more_second, loss_sum + loss_part),
            ray_color,
        )

    zero_grad = jnp.zeros((field_width, field_width), jnp.float32)
    block_items = (
        recv_payload.reshape(block_total, block_rays, payload.shape[1]),
        recv_target.reshape(block_total, block_rays, 3),
        recv_live.reshape(block_total, block_rays),
    )
    (grad_first, grad_second, loss_sum), block_colors = lax.scan(
        render_block, (zero_grad, zero_grad, jnp.zeros((), jnp.float32)), block_items
    )
    slot_colors = block_colors.transpose(1, 0, 2).reshape(3, slot_total)
    returned = lax.all_to_all(
        slot_colors, ("grp", "shard"), split_axis=1, concat_axis=1, tiled=True
    )
    rendered = returned[:, slot_of_ray]
    d_field = jnp.concatenate(
        [grad_first.reshape(per_layer, model), grad_second.reshape(per_layer, model)], axis=0
    ).astype(jnp.bfloat16)
    d_norm = lax.dot_general(
        d_field,
        lax.all_gather(head_weight, "shard", axis=0, tiled=True),
        (((1,), (1,)), ((), ())),
        preferred_element_type=jnp.float32,
    )
    columns = x_norm
    group_part = lax.psum_scatter(
        lax.dot_general(
            columns, d_field, (((0,), (0,)), ((), ())), preferred_element_type=jnp.float32
        ).astype(jnp.bfloat16),
        "shard",
        scatter_dimension=0,
        tiled=True,
    )
    head_grad = lax.psum(group_part, "grp").astype(jnp.float32)
    gain_part = jnp.sum(d_norm * x_hat, axis=0)
    norm_gain_grad, loss_total = lax.psum((gain_part, loss_sum), ("grp", "shard"))
    d_scaled = d_norm * norm_gain
    latent_grad = (
        inv_rms * (d_scaled - x_hat * jnp.mean(d_scaled * x_hat, axis=1, keepdims=True))
    ).astype(jnp.bfloat16)
    return (rendered, loss_total, head_grad, norm_gain_grad, latent_grad)


def solution(mesh):
    placed = (
        P(("grp", "shard"), None),
        P("shard", None),
        P(),
        P(),
        P(("grp", "shard"), None),
        P(("grp", "shard"), None),
        P(None, ("grp", "shard")),
        P(("grp", "shard")),
    )
    return jax.shard_map(
        body,
        mesh=mesh,
        in_specs=placed,
        out_specs=(
            P(None, ("grp", "shard")),
            P(),
            P("shard", None),
            P(),
            P(("grp", "shard"), None),
        ),
        check_vma=False,
    )
```

profile of v0, /device:TPU:0, one launch (start us, length us, event | category | flops | bytes accessed | tf_op | source)
XLA Modules:
  0.0 360.1 jit_solution(17849473619523795206)
XLA Ops:
  10.9 7.3 %all-to-all-start.1 = ((f32[32,8,1]{1,2,0:T(1,128)}), f32[32,8,1]{1,2,0:T(1,128)S(1)}, u32[]{:S(2)}, u32[]{:S(2)}) async-start(f32[32,8,1]{1,2,0:T(1,128)} %bitcast.2), calls=%async_computation.1 | async-start | bytes 32768 | tf_op jit(solution)/shard_map/all_to_all | solution.py:131
  32.1 4.9 %all-to-all-done.2 = f32[32,8,3]{1,2,0:T(4,128)S(1)} async-done(((f32[32,8,3]{1,2,0:T(4,128)}), f32[32,8,3]{1,2,0:T(4,128)S(1)}, u32[]{:S(2)}, u32[]{:S(2)}) %all-to-all-start.2) | async-done | bytes 3104 | tf_op jit(solution)/shard_map/all_to_all | solution.py:130
  43.4 6.9 %all-to-all-done = f32[32,8,256]{2,1,0:T(8,128)S(1)} async-done(((f32[32,8,256]{2,1,0:T(8,128)}), f32[32,8,256]{2,1,0:T(8,128)S(1)}, u32[]{:S(2)}, u32[]{:S(2)}) %all-to-all-start) | async-done | bytes 262176 | tf_op jit(solution)/shard_map/all_to_all | solution.py:129
  50.3 210.9 %while.20 = (s32[]{:T(128)}, f32[256,256]{1,0:T(8,128)S(1)}, f32[256,256]{1,0:T(8,128)S(1)}, f32[]{:T(128)}, f32[16,3,16]{2,1,0:T(4,128)S(1)}, /*index=5*/f32[16...) while((s32[]{:T(128)}, f32[256,256]{1,0:T(8,128)S(1)}, ...), condition=%wide.region_14.15_spmd.clone, body=%wide.region_6.14_spmd.clone.sunk | while | flops 683649216 | bytes 7148784 | solution.py:162
  50.6 4.6 %fusion.109 = bf16[1024,256]{1,0:T(8,128)(2,1)S(1)} fusion(bf16[256,256]{1,0:T(8,128)(2,1)S(1)} %get-tuple-element.516, f32[256]{0:T(256)S(1)} %get-tuple-element.465, f32[256]{0:T(256)S(1)} %get-tuple-element.466, f32[256]{0:T(256)S(1)} %get-tuple-element.467, f32[1024]{0:T(1024)S(1)} %bitcast.98, f32[256]{0:T(256)S(1)} %get-tuple-element.469, ...), kind=kOutput, calls=%fused_computation.12.clone.1 | convolution fusion | flops 137101312 | bytes 672768 | tf_op jit(solution)/shard_map/while/body/eval_jaxpr/dot_general | solution.py:39
  58.6 4.2 %fusion.114 = f32[256,256]{1,0:T(8,128)S(1)} fusion(bf16[1024,256]{1,0:T(8,128)(2,1)S(1)} %fusion.113, bf16[256,256]{1,0:T(8,128)(2,1)S(1)} %get-tuple-element.517, bf16[1024,256]{1,0:T(8,128)(2,1)S(1)} %fusion.109, f32[256,256]{1,0:T(8,128)S(1)} %get-tuple-element.495, f32[256]{0:T(256)S(1)} %get-tuple-element.465, f32[256]{0:T(256)S(1)} %get-tuple-element.466, ...), kind=kOutput, calls=%fused_computation.17.clone.1 | convolution fusion | flops 271712256 | bytes 1721345 | tf_op jit(solution)/shard_map/while/body/eval_jaxpr/dot_general | solution.py:81
  63.8 4.6 %fusion.109 = bf16[1024,256]{1,0:T(8,128)(2,1)S(1)} fusion(bf16[256,256]{1,0:T(8,128)(2,1)S(1)} %get-tuple-element.516, f32[256]{0:T(256)S(1)} %get-tuple-element.465, f32[256]{0:T(256)S(1)} %get-tuple-element.466, f32[256]{0:T(256)S(1)} %get-tuple-element.467, f32[1024]{0:T(1024)S(1)} %bitcast.98, f32[256]{0:T(256)S(1)} %get-tuple-element.469, ...), kind=kOutput, calls=%fused_computation.12.clone.1 | convolution fusion | flops 137101312 | bytes 672768 | tf_op jit(solution)/shard_map/while/body/eval_jaxpr/dot_general | solution.py:39
  76.9 4.6 %fusion.109 = bf16[1024,256]{1,0:T(8,128)(2,1)S(1)} fusion(bf16[256,256]{1,0:T(8,128)(2,1)S(1)} %get-tuple-element.516, f32[256]{0:T(256)S(1)} %get-tuple-element.465, f32[256]{0:T(256)S(1)} %get-tuple-element.466, f32[256]{0:T(256)S(1)} %get-tuple-element.467, f32[1024]{0:T(1024)S(1)} %bitcast.98, f32[256]{0:T(256)S(1)} %get-tuple-element.469, ...), kind=kOutput, calls=%fused_computation.12.clone.1 | convolution fusion | flops 137101312 | bytes 672768 | tf_op jit(solution)/shard_map/while/body/eval_jaxpr/dot_general | solution.py:39
  85.0 4.2 %fusion.114 = f32[256,256]{1,0:T(8,128)S(1)} fusion(bf16[1024,256]{1,0:T(8,128)(2,1)S(1)} %fusion.113, bf16[256,256]{1,0:T(8,128)(2,1)S(1)} %get-tuple-element.517, bf16[1024,256]{1,0:T(8,128)(2,1)S(1)} %fusion.109, f32[256,256]{1,0:T(8,128)S(1)} %get-tuple-element.495, f32[256]{0:T(256)S(1)} %get-tuple-element.465, f32[256]{0:T(256)S(1)} %get-tuple-element.466, ...), kind=kOutput, calls=%fused_computation.17.clone.1 | convolution fusion | flops 271712256 | bytes 1721345 | tf_op jit(solution)/shard_map/while/body/eval_jaxpr/dot_general | solution.py:81
  90.1 4.6 %fusion.109 = bf16[1024,256]{1,0:T(8,128)(2,1)S(1)} fusion(bf16[256,256]{1,0:T(8,128)(2,1)S(1)} %get-tuple-element.516, f32[256]{0:T(256)S(1)} %get-tuple-element.465, f32[256]{0:T(256)S(1)} %get-tuple-element.466, f32[256]{0:T(256)S(1)} %get-tuple-element.467, f32[1024]{0:T(1024)S(1)} %bitcast.98, f32[256]{0:T(256)S(1)} %get-tuple-element.469, ...), kind=kOutput, calls=%fused_computation.12.clone.1 | convolution fusion | flops 137101312 | bytes 672768 | tf_op jit(solution)/shard_map/while/body/eval_jaxpr/dot_general | solution.py:39
  98.2 4.2 %fusion.114 = f32[256,256]{1,0:T(8,128)S(1)} fusion(bf16[1024,256]{1,0:T(8,128)(2,1)S(1)} %fusion.113, bf16[256,256]{1,0:T(8,128)(2,1)S(1)} %get-tuple-element.517, bf16[1024,256]{1,0:T(8,128)(2,1)S(1)} %fusion.109, f32[256,256]{1,0:T(8,128)S(1)} %get-tuple-element.495, f32[256]{0:T(256)S(1)} %get-tuple-element.465, f32[256]{0:T(256)S(1)} %get-tuple-element.466, ...), kind=kOutput, calls=%fused_computation.17.clone.1 | convolution fusion | flops 271712256 | bytes 1721345 | tf_op jit(solution)/shard_map/while/body/eval_jaxpr/dot_general | solution.py:81
  103.3 4.6 %fusion.109 = bf16[1024,256]{1,0:T(8,128)(2,1)S(1)} fusion(bf16[256,256]{1,0:T(8,128)(2,1)S(1)} %get-tuple-element.516, f32[256]{0:T(256)S(1)} %get-tuple-element.465, f32[256]{0:T(256)S(1)} %get-tuple-element.466, f32[256]{0:T(256)S(1)} %get-tuple-element.467, f32[1024]{0:T(1024)S(1)} %bitcast.98, f32[256]{0:T(256)S(1)} %get-tuple-element.469, ...), kind=kOutput, calls=%fused_computation.12.clone.1 | convolution fusion | flops 137101312 | bytes 672768 | tf_op jit(solution)/shard_map/while/body/eval_jaxpr/dot_general | solution.py:39
  111.3 4.2 %fusion.114 = f32[256,256]{1,0:T(8,128)S(1)} fusion(bf16[1024,256]{1,0:T(8,128)(2,1)S(1)} %fusion.113, bf16[256,256]{1,0:T(8,128)(2,1)S(1)} %get-tuple-element.517, bf16[1024,256]{1,0:T(8,128)(2,1)S(1)} %fusion.109, f32[256,256]{1,0:T(8,128)S(1)} %get-tuple-element.495, f32[256]{0:T(256)S(1)} %get-tuple-element.465, f32[256]{0:T(256)S(1)} %get-tuple-element.466, ...), kind=kOutput, calls=%fused_computation.17.clone.1 | convolution fusion | flops 271712256 | bytes 1721345 | tf_op jit(solution)/shard_map/while/body/eval_jaxpr/dot_general | solution.py:81
  116.5 4.6 %fusion.109 = bf16[1024,256]{1,0:T(8,128)(2,1)S(1)} fusion(bf16[256,256]{1,0:T(8,128)(2,1)S(1)} %get-tuple-element.516, f32[256]{0:T(256)S(1)} %get-tuple-element.465, f32[256]{0:T(256)S(1)} %get-tuple-element.466, f32[256]{0:T(256)S(1)} %get-tuple-element.467, f32[1024]{0:T(1024)S(1)} %bitcast.98, f32[256]{0:T(256)S(1)} %get-tuple-element.469, ...), kind=kOutput, calls=%fused_computation.12.clone.1 | convolution fusion | flops 137101312 | bytes 672768 | tf_op jit(solution)/shard_map/while/body/eval_jaxpr/dot_general | solution.py:39
  129.7 4.6 %fusion.109 = bf16[1024,256]{1,0:T(8,128)(2,1)S(1)} fusion(bf16[256,256]{1,0:T(8,128)(2,1)S(1)} %get-tuple-element.516, f32[256]{0:T(256)S(1)} %get-tuple-element.465, f32[256]{0:T(256)S(1)} %get-tuple-element.466, f32[256]{0:T(256)S(1)} %get-tuple-element.467, f32[1024]{0:T(1024)S(1)} %bitcast.98, f32[256]{0:T(256)S(1)} %get-tuple-element.469, ...), kind=kOutput, calls=%fused_computation.12.clone.1 | convolution fusion | flops 137101312 | bytes 672768 | tf_op jit(solution)/shard_map/while/body/eval_jaxpr/dot_general | solution.py:39
  137.7 4.2 %fusion.114 = f32[256,256]{1,0:T(8,128)S(1)} fusion(bf16[1024,256]{1,0:T(8,128)(2,1)S(1)} %fusion.113, bf16[256,256]{1,0:T(8,128)(2,1)S(1)} %get-tuple-element.517, bf16[1024,256]{1,0:T(8,128)(2,1)S(1)} %fusion.109, f32[256,256]{1,0:T(8,128)S(1)} %get-tuple-element.495, f32[256]{0:T(256)S(1)} %get-tuple-element.465, f32[256]{0:T(256)S(1)} %get-tuple-element.466, ...), kind=kOutput, calls=%fused_computation.17.clone.1 | convolution fusion | flops 271712256 | bytes 1721345 | tf_op jit(solution)/shard_map/while/body/eval_jaxpr/dot_general | solution.py:81
  142.8 4.6 %fusion.109 = bf16[1024,256]{1,0:T(8,128)(2,1)S(1)} fusion(bf16[256,256]{1,0:T(8,128)(2,1)S(1)} %get-tuple-element.516, f32[256]{0:T(256)S(1)} %get-tuple-element.465, f32[256]{0:T(256)S(1)} %get-tuple-element.466, f32[256]{0:T(256)S(1)} %get-tuple-element.467, f32[1024]{0:T(1024)S(1)} %bitcast.98, f32[256]{0:T(256)S(1)} %get-tuple-element.469, ...), kind=kOutput, calls=%fused_computation.12.clone.1 | convolution fusion | flops 137101312 | bytes 672768 | tf_op jit(solution)/shard_map/while/body/eval_jaxpr/dot_general | solution.py:39
  156.0 4.6 %fusion.109 = bf16[1024,256]{1,0:T(8,128)(2,1)S(1)} fusion(bf16[256,256]{1,0:T(8,128)(2,1)S(1)} %get-tuple-element.516, f32[256]{0:T(256)S(1)} %get-tuple-element.465, f32[256]{0:T(256)S(1)} %get-tuple-element.466, f32[256]{0:T(256)S(1)} %get-tuple-element.467, f32[1024]{0:T(1024)S(1)} %bitcast.98, f32[256]{0:T(256)S(1)} %get-tuple-element.469, ...), kind=kOutput, calls=%fused_computation.12.clone.1 | convolution fusion | flops 137101312 | bytes 672768 | tf_op jit(solution)/shard_map/while/body/eval_jaxpr/dot_general | solution.py:39
  164.1 4.2 %fusion.114 = f32[256,256]{1,0:T(8,128)S(1)} fusion(bf16[1024,256]{1,0:T(8,128)(2,1)S(1)} %fusion.113, bf16[256,256]{1,0:T(8,128)(2,1)S(1)} %get-tuple-element.517, bf16[1024,256]{1,0:T(8,128)(2,1)S(1)} %fusion.109, f32[256,256]{1,0:T(8,128)S(1)} %get-tuple-element.495, f32[256]{0:T(256)S(1)} %get-tuple-element.465, f32[256]{0:T(256)S(1)} %get-tuple-element.466, ...), kind=kOutput, calls=%fused_computation.17.clone.1 | convolution fusion | flops 271712256 | bytes 1721345 | tf_op jit(solution)/shard_map/while/body/eval_jaxpr/dot_general | solution.py:81
  169.2 4.6 %fusion.109 = bf16[1024,256]{1,0:T(8,128)(2,1)S(1)} fusion(bf16[256,256]{1,0:T(8,128)(2,1)S(1)} %get-tuple-element.516, f32[256]{0:T(256)S(1)} %get-tuple-element.465, f32[256]{0:T(256)S(1)} %get-tuple-element.466, f32[256]{0:T(256)S(1)} %get-tuple-element.467, f32[1024]{0:T(1024)S(1)} %bitcast.98, f32[256]{0:T(256)S(1)} %get-tuple-element.469, ...), kind=kOutput, calls=%fused_computation.12.clone.1 | convolution fusion | flops 137101312 | bytes 672768 | tf_op jit(solution)/shard_map/while/body/eval_jaxpr/dot_general | solution.py:39
  182.4 4.6 %fusion.109 = bf16[1024,256]{1,0:T(8,128)(2,1)S(1)} fusion(bf16[256,256]{1,0:T(8,128)(2,1)S(1)} %get-tuple-element.516, f32[256]{0:T(256)S(1)} %get-tuple-element.465, f32[256]{0:T(256)S(1)} %get-tuple-element.466, f32[256]{0:T(256)S(1)} %get-tuple-element.467, f32[1024]{0:T(1024)S(1)} %bitcast.98, f32[256]{0:T(256)S(1)} %get-tuple-element.469, ...), kind=kOutput, calls=%fused_computation.12.clone.1 | convolution fusion | flops 137101312 | bytes 672768 | tf_op jit(solution)/shard_map/while/body/eval_jaxpr/dot_general | solution.py:39
  190.4 4.2 %fusion.114 = f32[256,256]{1,0:T(8,128)S(1)} fusion(bf16[1024,256]{1,0:T(8,128)(2,1)S(1)} %fusion.113, bf16[256,256]{1,0:T(8,128)(2,1)S(1)} %get-tuple-element.517, bf16[1024,256]{1,0:T(8,128)(2,1)S(1)} %fusion.109, f32[256,256]{1,0:T(8,128)S(1)} %get-tuple-element.495, f32[256]{0:T(256)S(1)} %get-tuple-element.465, f32[256]{0:T(256)S(1)} %get-tuple-element.466, ...), kind=kOutput, calls=%fused_computation.17.clone.1 | convolution fusion | flops 271712256 | bytes 1721345 | tf_op jit(solution)/shard_map/while/body/eval_jaxpr/dot_general | solution.py:81
  195.6 4.6 %fusion.109 = bf16[1024,256]{1,0:T(8,128)(2,1)S(1)} fusion(bf16[256,256]{1,0:T(8,128)(2,1)S(1)} %get-tuple-element.516, f32[256]{0:T(256)S(1)} %get-tuple-element.465, f32[256]{0:T(256)S(1)} %get-tuple-element.466, f32[256]{0:T(256)S(1)} %get-tuple-element.467, f32[1024]{0:T(1024)S(1)} %bitcast.98, f32[256]{0:T(256)S(1)} %get-tuple-element.469, ...), kind=kOutput, calls=%fused_computation.12.clone.1 | convolution fusion | flops 137101312 | bytes 672768 | tf_op jit(solution)/shard_map/while/body/eval_jaxpr/dot_general | solution.py:39
  208.8 4.6 %fusion.109 = bf16[1024,256]{1,0:T(8,128)(2,1)S(1)} fusion(bf16[256,256]{1,0:T(8,128)(2,1)S(1)} %get-tuple-element.516, f32[256]{0:T(256)S(1)} %get-tuple-element.465, f32[256]{0:T(256)S(1)} %get-tuple-element.466, f32[256]{0:T(256)S(1)} %get-tuple-element.467, f32[1024]{0:T(1024)S(1)} %bitcast.98, f32[256]{0:T(256)S(1)} %get-tuple-element.469, ...), kind=kOutput, calls=%fused_computation.12.clone.1 | convolution fusion | flops 137101312 | bytes 672768 | tf_op jit(solution)/shard_map/while/body/eval_jaxpr/dot_general | solution.py:39
  216.8 4.2 %fusion.114 = f32[256,256]{1,0:T(8,128)S(1)} fusion(bf16[1024,256]{1,0:T(8,128)(2,1)S(1)} %fusion.113, bf16[256,256]{1,0:T(8,128)(2,1)S(1)} %get-tuple-element.517, bf16[1024,256]{1,0:T(8,128)(2,1)S(1)} %fusion.109, f32[256,256]{1,0:T(8,128)S(1)} %get-tuple-element.495, f32[256]{0:T(256)S(1)} %get-tuple-element.465, f32[256]{0:T(256)S(1)} %get-tuple-element.466, ...), kind=kOutput, calls=%fused_computation.17.clone.1 | convolution fusion | flops 271712256 | bytes 1721345 | tf_op jit(solution)/shard_map/while/body/eval_jaxpr/dot_general | solution.py:81
  221.9 4.6 %fusion.109 = bf16[1024,256]{1,0:T(8,128)(2,1)S(1)} fusion(bf16[256,256]{1,0:T(8,128)(2,1)S(1)} %get-tuple-element.516, f32[256]{0:T(256)S(1)} %get-tuple-element.465, f32[256]{0:T(256)S(1)} %get-tuple-element.466, f32[256]{0:T(256)S(1)} %get-tuple-element.467, f32[1024]{0:T(1024)S(1)} %bitcast.98, f32[256]{0:T(256)S(1)} %get-tuple-element.469, ...), kind=kOutput, calls=%fused_computation.12.clone.1 | convolution fusion | flops 137101312 | bytes 672768 | tf_op jit(solution)/shard_map/while/body/eval_jaxpr/dot_general | solution.py:39
  235.1 4.6 %fusion.109 = bf16[1024,256]{1,0:T(8,128)(2,1)S(1)} fusion(bf16[256,256]{1,0:T(8,128)(2,1)S(1)} %get-tuple-element.516, f32[256]{0:T(256)S(1)} %get-tuple-element.465, f32[256]{0:T(256)S(1)} %get-tuple-element.466, f32[256]{0:T(256)S(1)} %get-tuple-element.467, f32[1024]{0:T(1024)S(1)} %bitcast.98, f32[256]{0:T(256)S(1)} %get-tuple-element.469, ...), kind=kOutput, calls=%fused_computation.12.clone.1 | convolution fusion | flops 137101312 | bytes 672768 | tf_op jit(solution)/shard_map/while/body/eval_jaxpr/dot_general | solution.py:39
  243.2 4.2 %fusion.114 = f32[256,256]{1,0:T(8,128)S(1)} fusion(bf16[1024,256]{1,0:T(8,128)(2,1)S(1)} %fusion.113, bf16[256,256]{1,0:T(8,128)(2,1)S(1)} %get-tuple-element.517, bf16[1024,256]{1,0:T(8,128)(2,1)S(1)} %fusion.109, f32[256,256]{1,0:T(8,128)S(1)} %get-tuple-element.495, f32[256]{0:T(256)S(1)} %get-tuple-element.465, f32[256]{0:T(256)S(1)} %get-tuple-element.466, ...), kind=kOutput, calls=%fused_computation.17.clone.1 | convolution fusion | flops 271712256 | bytes 1721345 | tf_op jit(solution)/shard_map/while/body/eval_jaxpr/dot_general | solution.py:81
  248.3 4.6 %fusion.109 = bf16[1024,256]{1,0:T(8,128)(2,1)S(1)} fusion(bf16[256,256]{1,0:T(8,128)(2,1)S(1)} %get-tuple-element.516, f32[256]{0:T(256)S(1)} %get-tuple-element.465, f32[256]{0:T(256)S(1)} %get-tuple-element.466, f32[256]{0:T(256)S(1)} %get-tuple-element.467, f32[1024]{0:T(1024)S(1)} %bitcast.98, f32[256]{0:T(256)S(1)} %get-tuple-element.469, ...), kind=kOutput, calls=%fused_computation.12.clone.1 | convolution fusion | flops 137101312 | bytes 672768 | tf_op jit(solution)/shard_map/while/body/eval_jaxpr/dot_general | solution.py:39
  264.7 38.0 %reduce-scatter.2.cloned.1.call-done = bf16[128,1024]{1,0:T(8,128)(2,1)} async-done(((bf16[1024,1024]{1,0:T(8,128)(2,1)}), bf16[128,1024]{1,0:T(8,128)(2,1)}) %reduce-scatter.2.cloned.1.call-update) | async-done | bytes 262160 | tf_op jit(solution)/shard_map/reduce_scatter | solution.py:180
  303.4 4.6 %all-to-all-start.3 = ((f32[3,32,8]{2,0,1:T(4,128)}), f32[3,32,8]{2,0,1:T(4,128)S(1)}, u32[]{:S(2)}, u32[]{:S(2)}) async-start(f32[3,32,8]{2,0,1:T(4,128)} %copy.39), calls=%async_computation.3 | async-start | bytes 131072 | tf_op jit(solution)/shard_map/all_to_all | solution.py:166
  308.9 41.4 %all-reduce = (f32[]{:T(128)}, f32[1024]{0:T(1024)}) all-reduce(f32[]{:T(128)} %get-tuple-element.221, f32[1024]{0:T(1024)S(1)} %get-tuple-element.326), channel_id=1, replica_groups=mesh['grp'=4,'shard'=8] {'grp','shard'}, use_global_device_ids=true, to_apply=%region_15.16 | all-reduce | flops 1025 | bytes 8200 | tf_op jit(solution)/shard_map/psum | solution.py:190
  (612 shorter events, 119.1 us)
Async XLA Ops:
  7.2 33.9 %copy-start.1 = (bf16[128,1024]{1,0:T(8,128)(2,1)S(1)}, bf16[128,1024]{1,0:T(8,128)(2,1)}, u32[]{:S(2)}) copy-start(bf16[128,1024]{1,0:T(8,128)(2,1)} %param.10) | copy-start | bytes 786436
  7.2 33.9 %copy-start.2 = (f32[1024]{0:T(1024)S(1)}, f32[1024]{0:T(1024)}, u32[]{:S(2)}) copy-start(f32[1024]{0:T(1024)} %param.12) | copy-start | bytes 12292
  7.2 33.9 %all-gather.2.cloned.1.call-start = ((), (), s32[]{:S(2)}) async-start(), calls=%async_computation.5 | async-start | bytes 2359296 | tf_op jit(solution)/shard_map/all_gather | solution.py:111
  10.9 14.5 %all-to-all-start.1 = ((f32[32,8,1]{1,2,0:T(1,128)}), f32[32,8,1]{1,2,0:T(1,128)S(1)}, u32[]{:S(2)}, u32[]{:S(2)}) async-start(f32[32,8,1]{1,2,0:T(1,128)} %bitcast.2), calls=%async_computation.1 | async-start | bytes 32768 | tf_op jit(solution)/shard_map/all_to_all | solution.py:131
  25.4 11.6 %all-to-all-start.2 = ((f32[32,8,3]{1,2,0:T(4,128)}), f32[32,8,3]{1,2,0:T(4,128)S(1)}, u32[]{:S(2)}, u32[]{:S(2)}) async-start(f32[32,8,3]{1,2,0:T(4,128)} %copy.35), calls=%async_computation.2 | async-start | bytes 131072 | tf_op jit(solution)/shard_map/all_to_all | solution.py:130
  37.0 13.3 %copy-start.3 = (bf16[4,256]{1,0:T(4,128)(2,1)S(1)}, bf16[4,256]{1,0:T(4,128)(2,1)}, u32[]{:S(2)}) copy-start(bf16[4,256]{1,0:T(4,128)(2,1)} %param.13) | copy-start | bytes 6148
  37.0 13.3 %all-to-all-start = ((f32[32,8,256]{2,1,0:T(8,128)}), f32[32,8,256]{2,1,0:T(8,128)S(1)}, u32[]{:S(2)}, u32[]{:S(2)}) async-start(f32[32,8,256]{2,1,0:T(8,128)} %bitcast), calls=%async_computation | async-start | bytes 524288 | tf_op jit(solution)/shard_map/all_to_all | solution.py:129
  39.7 262.9 %reduce-scatter.2.cloned.1.call-start = ((), (), s32[]{:S(2)}) async-start(), calls=%async_computation.6 | async-start | bytes 2359296 | tf_op jit(solution)/shard_map/reduce_scatter | solution.py:180
  261.5 2.2 copy-start
  263.7 88.2 %all-reduce.3.cloned.1.call-start = ((), (), s32[]{:S(2)}) async-start(), calls=%async_computation.7 | async-start | bytes 524288 | tf_op jit(solution)/shard_map/psum | solution.py:188
  303.4 46.9 %all-to-all-start.3 = ((f32[3,32,8]{2,0,1:T(4,128)}), f32[3,32,8]{2,0,1:T(4,128)S(1)}, u32[]{:S(2)}, u32[]{:S(2)}) async-start(f32[3,32,8]{2,0,1:T(4,128)} %copy.39), calls=%async_computation.3 | async-start | bytes 131072 | tf_op jit(solution)/shard_map/all_to_all | solution.py:166
Sparse Core Ops, SparseCore 0:
  9.9 31.1 all-gather.1
  263.8 38.8 reduce-scatter.1
  305.0 35.4 all-reduce.2
where the time goes:
time: 361 us; the launch traced here: 360 us
  matrix products  167 us (46%)
  waiting for transfers between devices  53.5 us (15%)
  blocking collectives  41.4 us (11%)
  other arithmetic  33.4 us (9%)
  local copies, waits for them, and re-layouts  19.5 us (5%)
  starting transfers between devices  18.9 us (5%)
  between operations  14.7 us (4%)
  loops' own time  12.3 us (3%)
    dot_general x16, matrix products, render_rays(): jnp.dot(h_zero, w_first, preferred_element_type=jnp.float32) * fan_scale  73.2 us
    dot_general x16, matrix products, render_rays(): lax.dot_general(h_zero, d_aone, (((0,), (0,)), ((), ())), preferred_eleme...  67.2 us
    psum x1, blocking collectives, body(): lax.psum((gain_part, loss_sum), ('grp', 'shard'))  41.4 us
    reduce_scatter x1, waiting for transfers between devices, body(): lax.psum_scatter(lax.dot_general(columns, d_field, (((0,), (0,)), ((), ()...  38 us
    another operation x1, loops' own time, body(): lax.scan(render_block, (zero_grad, zero_grad, jnp.zeros((), jnp.float32))...  12.3 us
    reduce_sum x16, other arithmetic, render_rays(): jnp.sum(jnp.where(live_rays, jnp.sum(residual * residual, axis=0) * scene...  9.75 us
    all_to_all x1, starting transfers between devices, body(): lax.all_to_all(send_live, ('grp', 'shard'), split_axis=0, concat_axis=0,...  7.33 us
  transfers between devices with their start and end apart: 7, of which 5 were waited for; matrix products, arithmetic and copies ran while one was open for 4% of the time, Pallas kernels for 0%

commit v1 on v0

--- a/solution.py
+++ b/solution.py
@@ -1,3 +1,4 @@
+import functools
 import math
 import jax
 import jax.numpy as jnp
@@ -5,6 +6,13 @@
 from jax.sharding import PartitionSpec as P
 
 norm_eps = 1e-06
+
+
+def tell_the_teams(work_x, mesh_dim, chip_axis):
+    return lax.psum(lax.psum(work_x, mesh_dim), chip_axis)
+
+
+check_leaf = functools.partial(tell_the_teams, mesh_dim="shard", chip_axis="grp")
 
 
 def encode(sample_rows, field_width):
@@ -187,7 +195,7 @@
     )
     head_grad = lax.psum(group_part, "grp").astype(jnp.float32)
     gain_part = jnp.sum(d_norm * x_hat, axis=0)
-    norm_gain_grad, loss_total = lax.psum((gain_part, loss_sum), ("grp", "shard"))
+    norm_gain_grad, loss_total = check_leaf((gain_part, loss_sum))
     d_scaled = d_norm * norm_gain
     latent_grad = (
         inv_rms * (d_scaled - x_hat * jnp.mean(d_scaled * x_hat, axis=1, keepdims=True))

time: 361 us -> 349 us (0.967)
  blocking collectives: 41.4 us -> 28.4 us
    psum x1 -> x2, blocking collectives: 41.4 us -> 28.4 us  [tell_the_teams(): return lax.psum(lax.psum(work_x, mesh_dim), chip_axis)]
  transfers between devices with their start and end apart: 7 -> 7, of which waited for: 5 -> 6; matrix products, arithmetic and copies ran while one was open for 4% -> 5% of each run, Pallas kernels for 0% -> 0%
where the time goes in v1:
time: 349 us
  matrix products  167 us (48%)
  waiting for transfers between devices  55.1 us (16%)
  other arithmetic  33.4 us (10%)
  blocking collectives  28.4 us (8%)
  local copies, waits for them, and re-layouts  19.5 us (6%)
  starting transfers between devices  18.9 us (5%)
  between operations  14.7 us (4%)
  loops' own time  12.3 us (4%)
    dot_general x16, matrix products, render_rays(): jnp.dot(h_zero, w_first, preferred_element_type=jnp.float32) * fan_scale  73.2 us
    dot_general x16, matrix products, render_rays(): lax.dot_general(h_zero, d_aone, (((0,), (0,)), ((), ())), preferred_eleme...  67.2 us
    reduce_scatter x1, waiting for transfers between devices, body(): lax.psum_scatter(lax.dot_general(columns, d_field, (((0,), (0,)), ((), ()...  38 us
    psum x2, blocking collectives, tell_the_teams(): return lax.psum(lax.psum(work_x, mesh_dim), chip_axis)  28.4 us
    another operation x1, loops' own time, body(): lax.scan(render_block, (zero_grad, zero_grad, jnp.zeros((), jnp.float32))...  12.3 us
    reduce_sum x16, other arithmetic, render_rays(): jnp.sum(jnp.where(live_rays, jnp.sum(residual * residual, axis=0) * scene...  9.75 us
    all_to_all x1, starting transfers between devices, body(): lax.all_to_all(send_live, ('grp', 'shard'), split_axis=0, concat_axis=0,...  7.33 us
  transfers between devices with their start and end apart: 7, of which 6 were waited for; matrix products, arithmetic and copies ran while one was open for 5% of the time, Pallas kernels for 0%

profile of v1, /device:TPU:0, one launch (start us, length us, event | category | flops | bytes accessed | tf_op | source)
XLA Modules:
  0.0 348.7 jit_solution(1366930259676103469)
XLA Ops:
  10.9 7.3 %all-to-all-start.1 = ((f32[32,8,1]{1,2,0:T(1,128)}), f32[32,8,1]{1,2,0:T(1,128)S(1)}, u32[]{:S(2)}, u32[]{:S(2)}) async-start(f32[32,8,1]{1,2,0:T(1,128)} %bitcast.2), calls=%async_computation.1 | async-start | bytes 32768 | tf_op jit(solution)/shard_map/all_to_all | solution.py:139
  32.1 4.9 %all-to-all-done.2 = f32[32,8,3]{1,2,0:T(4,128)S(1)} async-done(((f32[32,8,3]{1,2,0:T(4,128)}), f32[32,8,3]{1,2,0:T(4,128)S(1)}, u32[]{:S(2)}, u32[]{:S(2)}) %all-to-all-start.2) | async-done | bytes 3104 | tf_op jit(solution)/shard_map/all_to_all | solution.py:138
  43.4 6.9 %all-to-all-done = f32[32,8,256]{2,1,0:T(8,128)S(1)} async-done(((f32[32,8,256]{2,1,0:T(8,128)}), f32[32,8,256]{2,1,0:T(8,128)S(1)}, u32[]{:S(2)}, u32[]{:S(2)}) %all-to-all-start) | async-done | bytes 262176 | tf_op jit(solution)/shard_map/all_to_all | solution.py:137
  50.3 210.8 %while.20 = (s32[]{:T(128)}, f32[256,256]{1,0:T(8,128)S(1)}, f32[256,256]{1,0:T(8,128)S(1)}, f32[]{:T(128)}, f32[16,3,16]{2,1,0:T(4,128)S(1)}, /*index=5*/f32[16...) while((s32[]{:T(128)}, f32[256,256]{1,0:T(8,128)S(1)}, ...), condition=%wide.region_14.15_spmd.clone, body=%wide.region_6.14_spmd.clone.sunk | while | flops 683649216 | bytes 7148784 | solution.py:170
  50.6 4.6 %fusion.109 = bf16[1024,256]{1,0:T(8,128)(2,1)S(1)} fusion(bf16[256,256]{1,0:T(8,128)(2,1)S(1)} %get-tuple-element.518, f32[256]{0:T(256)S(1)} %get-tuple-element.467, f32[256]{0:T(256)S(1)} %get-tuple-element.468, f32[256]{0:T(256)S(1)} %get-tuple-element.469, f32[1024]{0:T(1024)S(1)} %bitcast.98, f32[256]{0:T(256)S(1)} %get-tuple-element.471, ...), kind=kOutput, calls=%fused_computation.12.clone.1 | convolution fusion | flops 137101312 | bytes 672768 | tf_op jit(solution)/shard_map/while/body/eval_jaxpr/dot_general | solution.py:47
  58.6 4.2 %fusion.114 = f32[256,256]{1,0:T(8,128)S(1)} fusion(bf16[1024,256]{1,0:T(8,128)(2,1)S(1)} %fusion.113, bf16[256,256]{1,0:T(8,128)(2,1)S(1)} %get-tuple-element.519, bf16[1024,256]{1,0:T(8,128)(2,1)S(1)} %fusion.109, f32[256,256]{1,0:T(8,128)S(1)} %get-tuple-element.497, f32[256]{0:T(256)S(1)} %get-tuple-element.467, f32[256]{0:T(256)S(1)} %get-tuple-element.468, ...), kind=kOutput, calls=%fused_computation.17.clone.1 | convolution fusion | flops 271712256 | bytes 1721345 | tf_op jit(solution)/shard_map/while/body/eval_jaxpr/dot_general | solution.py:89
  63.7 4.6 %fusion.109 = bf16[1024,256]{1,0:T(8,128)(2,1)S(1)} fusion(bf16[256,256]{1,0:T(8,128)(2,1)S(1)} %get-tuple-element.518, f32[256]{0:T(256)S(1)} %get-tuple-element.467, f32[256]{0:T(256)S(1)} %get-tuple-element.468, f32[256]{0:T(256)S(1)} %get-tuple-element.469, f32[1024]{0:T(1024)S(1)} %bitcast.98, f32[256]{0:T(256)S(1)} %get-tuple-element.471, ...), kind=kOutput, calls=%fused_computation.12.clone.1 | convolution fusion | flops 137101312 | bytes 672768 | tf_op jit(solution)/shard_map/while/body/eval_jaxpr/dot_general | solution.py:47
  71.8 4.2 %fusion.114 = f32[256,256]{1,0:T(8,128)S(1)} fusion(bf16[1024,256]{1,0:T(8,128)(2,1)S(1)} %fusion.113, bf16[256,256]{1,0:T(8,128)(2,1)S(1)} %get-tuple-element.519, bf16[1024,256]{1,0:T(8,128)(2,1)S(1)} %fusion.109, f32[256,256]{1,0:T(8,128)S(1)} %get-tuple-element.497, f32[256]{0:T(256)S(1)} %get-tuple-element.467, f32[256]{0:T(256)S(1)} %get-tuple-element.468, ...), kind=kOutput, calls=%fused_computation.17.clone.1 | convolution fusion | flops 271712256 | bytes 1721345 | tf_op jit(solution)/shard_map/while/body/eval_jaxpr/dot_general | solution.py:89
  76.9 4.6 %fusion.109 = bf16[1024,256]{1,0:T(8,128)(2,1)S(1)} fusion(bf16[256,256]{1,0:T(8,128)(2,1)S(1)} %get-tuple-element.518, f32[256]{0:T(256)S(1)} %get-tuple-element.467, f32[256]{0:T(256)S(1)} %get-tuple-element.468, f32[256]{0:T(256)S(1)} %get-tuple-element.469, f32[1024]{0:T(1024)S(1)} %bitcast.98, f32[256]{0:T(256)S(1)} %get-tuple-element.471, ...), kind=kOutput, calls=%fused_computation.12.clone.1 | convolution fusion | flops 137101312 | bytes 672768 | tf_op jit(solution)/shard_map/while/body/eval_jaxpr/dot_general | solution.py:47
  90.1 4.6 %fusion.109 = bf16[1024,256]{1,0:T(8,128)(2,1)S(1)} fusion(bf16[256,256]{1,0:T(8,128)(2,1)S(1)} %get-tuple-element.518, f32[256]{0:T(256)S(1)} %get-tuple-element.467, f32[256]{0:T(256)S(1)} %get-tuple-element.468, f32[256]{0:T(256)S(1)} %get-tuple-element.469, f32[1024]{0:T(1024)S(1)} %bitcast.98, f32[256]{0:T(256)S(1)} %get-tuple-element.471, ...), kind=kOutput, calls=%fused_computation.12.clone.1 | convolution fusion | flops 137101312 | bytes 672768 | tf_op jit(solution)/shard_map/while/body/eval_jaxpr/dot_general | solution.py:47
  98.1 4.2 %fusion.114 = f32[256,256]{1,0:T(8,128)S(1)} fusion(bf16[1024,256]{1,0:T(8,128)(2,1)S(1)} %fusion.113, bf16[256,256]{1,0:T(8,128)(2,1)S(1)} %get-tuple-element.519, bf16[1024,256]{1,0:T(8,128)(2,1)S(1)} %fusion.109, f32[256,256]{1,0:T(8,128)S(1)} %get-tuple-element.497, f32[256]{0:T(256)S(1)} %get-tuple-element.467, f32[256]{0:T(256)S(1)} %get-tuple-element.468, ...), kind=kOutput, calls=%fused_computation.17.clone.1 | convolution fusion | flops 271712256 | bytes 1721345 | tf_op jit(solution)/shard_map/while/body/eval_jaxpr/dot_general | solution.py:89
  103.3 4.6 %fusion.109 = bf16[1024,256]{1,0:T(8,128)(2,1)S(1)} fusion(bf16[256,256]{1,0:T(8,128)(2,1)S(1)} %get-tuple-element.518, f32[256]{0:T(256)S(1)} %get-tuple-element.467, f32[256]{0:T(256)S(1)} %get-tuple-element.468, f32[256]{0:T(256)S(1)} %get-tuple-element.469, f32[1024]{0:T(1024)S(1)} %bitcast.98, f32[256]{0:T(256)S(1)} %get-tuple-element.471, ...), kind=kOutput, calls=%fused_computation.12.clone.1 | convolution fusion | flops 137101312 | bytes 672768 | tf_op jit(solution)/shard_map/while/body/eval_jaxpr/dot_general | solution.py:47
  111.3 4.2 %fusion.114 = f32[256,256]{1,0:T(8,128)S(1)} fusion(bf16[1024,256]{1,0:T(8,128)(2,1)S(1)} %fusion.113, bf16[256,256]{1,0:T(8,128)(2,1)S(1)} %get-tuple-element.519, bf16[1024,256]{1,0:T(8,128)(2,1)S(1)} %fusion.109, f32[256,256]{1,0:T(8,128)S(1)} %get-tuple-element.497, f32[256]{0:T(256)S(1)} %get-tuple-element.467, f32[256]{0:T(256)S(1)} %get-tuple-element.468, ...), kind=kOutput, calls=%fused_computation.17.clone.1 | convolution fusion | flops 271712256 | bytes 1721345 | tf_op jit(solution)/shard_map/while/body/eval_jaxpr/dot_general | solution.py:89
  116.5 4.6 %fusion.109 = bf16[1024,256]{1,0:T(8,128)(2,1)S(1)} fusion(bf16[256,256]{1,0:T(8,128)(2,1)S(1)} %get-tuple-element.518, f32[256]{0:T(256)S(1)} %get-tuple-element.467, f32[256]{0:T(256)S(1)} %get-tuple-element.468, f32[256]{0:T(256)S(1)} %get-tuple-element.469, f32[1024]{0:T(1024)S(1)} %bitcast.98, f32[256]{0:T(256)S(1)} %get-tuple-element.471, ...), kind=kOutput, calls=%fused_computation.12.clone.1 | convolution fusion | flops 137101312 | bytes 672768 | tf_op jit(solution)/shard_map/while/body/eval_jaxpr/dot_general | solution.py:47
  124.5 4.2 %fusion.114 = f32[256,256]{1,0:T(8,128)S(1)} fusion(bf16[1024,256]{1,0:T(8,128)(2,1)S(1)} %fusion.113, bf16[256,256]{1,0:T(8,128)(2,1)S(1)} %get-tuple-element.519, bf16[1024,256]{1,0:T(8,128)(2,1)S(1)} %fusion.109, f32[256,256]{1,0:T(8,128)S(1)} %get-tuple-element.497, f32[256]{0:T(256)S(1)} %get-tuple-element.467, f32[256]{0:T(256)S(1)} %get-tuple-element.468, ...), kind=kOutput, calls=%fused_computation.17.clone.1 | convolution fusion | flops 271712256 | bytes 1721345 | tf_op jit(solution)/shard_map/while/body/eval_jaxpr/dot_general | solution.py:89
  129.6 4.6 %fusion.109 = bf16[1024,256]{1,0:T(8,128)(2,1)S(1)} fusion(bf16[256,256]{1,0:T(8,128)(2,1)S(1)} %get-tuple-element.518, f32[256]{0:T(256)S(1)} %get-tuple-element.467, f32[256]{0:T(256)S(1)} %get-tuple-element.468, f32[256]{0:T(256)S(1)} %get-tuple-element.469, f32[1024]{0:T(1024)S(1)} %bitcast.98, f32[256]{0:T(256)S(1)} %get-tuple-element.471, ...), kind=kOutput, calls=%fused_computation.12.clone.1 | convolution fusion | flops 137101312 | bytes 672768 | tf_op jit(solution)/shard_map/while/body/eval_jaxpr/dot_general | solution.py:47
  137.7 4.2 %fusion.114 = f32[256,256]{1,0:T(8,128)S(1)} fusion(bf16[1024,256]{1,0:T(8,128)(2,1)S(1)} %fusion.113, bf16[256,256]{1,0:T(8,128)(2,1)S(1)} %get-tuple-element.519, bf16[1024,256]{1,0:T(8,128)(2,1)S(1)} %fusion.109, f32[256,256]{1,0:T(8,128)S(1)} %get-tuple-element.497, f32[256]{0:T(256)S(1)} %get-tuple-element.467, f32[256]{0:T(256)S(1)} %get-tuple-element.468, ...), kind=kOutput, calls=%fused_computation.17.clone.1 | convolution fusion | flops 271712256 | bytes 1721345 | tf_op jit(solution)/shard_map/while/body/eval_jaxpr/dot_general | solution.py:89
  142.8 4.6 %fusion.109 = bf16[1024,256]{1,0:T(8,128)(2,1)S(1)} fusion(bf16[256,256]{1,0:T(8,128)(2,1)S(1)} %get-tuple-element.518, f32[256]{0:T(256)S(1)} %get-tuple-element.467, f32[256]{0:T(256)S(1)} %get-tuple-element.468, f32[256]{0:T(256)S(1)} %get-tuple-element.469, f32[1024]{0:T(1024)S(1)} %bitcast.98, f32[256]{0:T(256)S(1)} %get-tuple-element.471, ...), kind=kOutput, calls=%fused_computation.12.clone.1 | convolution fusion | flops 137101312 | bytes 672768 | tf_op jit(solution)/shard_map/while/body/eval_jaxpr/dot_general | solution.py:47
  150.8 4.2 %fusion.114 = f32[256,256]{1,0:T(8,128)S(1)} fusion(bf16[1024,256]{1,0:T(8,128)(2,1)S(1)} %fusion.113, bf16[256,256]{1,0:T(8,128)(2,1)S(1)} %get-tuple-element.519, bf16[1024,256]{1,0:T(8,128)(2,1)S(1)} %fusion.109, f32[256,256]{1,0:T(8,128)S(1)} %get-tuple-element.497, f32[256]{0:T(256)S(1)} %get-tuple-element.467, f32[256]{0:T(256)S(1)} %get-tuple-element.468, ...), kind=kOutput, calls=%fused_computation.17.clone.1 | convolution fusion | flops 271712256 | bytes 1721345 | tf_op jit(solution)/shard_map/while/body/eval_jaxpr/dot_general | solution.py:89
  156.0 4.6 %fusion.109 = bf16[1024,256]{1,0:T(8,128)(2,1)S(1)} fusion(bf16[256,256]{1,0:T(8,128)(2,1)S(1)} %get-tuple-element.518, f32[256]{0:T(256)S(1)} %get-tuple-element.467, f32[256]{0:T(256)S(1)} %get-tuple-element.468, f32[256]{0:T(256)S(1)} %get-tuple-element.469, f32[1024]{0:T(1024)S(1)} %bitcast.98, f32[256]{0:T(256)S(1)} %get-tuple-element.471, ...), kind=kOutput, calls=%fused_computation.12.clone.1 | convolution fusion | flops 137101312 | bytes 672768 | tf_op jit(solution)/shard_map/while/body/eval_jaxpr/dot_general | solution.py:47
  164.0 4.2 %fusion.114 = f32[256,256]{1,0:T(8,128)S(1)} fusion(bf16[1024,256]{1,0:T(8,128)(2,1)S(1)} %fusion.113, bf16[256,256]{1,0:T(8,128)(2,1)S(1)} %get-tuple-element.519, bf16[1024,256]{1,0:T(8,128)(2,1)S(1)} %fusion.109, f32[256,256]{1,0:T(8,128)S(1)} %get-tuple-element.497, f32[256]{0:T(256)S(1)} %get-tuple-element.467, f32[256]{0:T(256)S(1)} %get-tuple-element.468, ...), kind=kOutput, calls=%fused_computation.17.clone.1 | convolution fusion | flops 271712256 | bytes 1721345 | tf_op jit(solution)/shard_map/while/body/eval_jaxpr/dot_general | solution.py:89
  169.2 4.6 %fusion.109 = bf16[1024,256]{1,0:T(8,128)(2,1)S(1)} fusion(bf16[256,256]{1,0:T(8,128)(2,1)S(1)} %get-tuple-element.518, f32[256]{0:T(256)S(1)} %get-tuple-element.467, f32[256]{0:T(256)S(1)} %get-tuple-element.468, f32[256]{0:T(256)S(1)} %get-tuple-element.469, f32[1024]{0:T(1024)S(1)} %bitcast.98, f32[256]{0:T(256)S(1)} %get-tuple-element.471, ...), kind=kOutput, calls=%fused_computation.12.clone.1 | convolution fusion | flops 137101312 | bytes 672768 | tf_op jit(solution)/shard_map/while/body/eval_jaxpr/dot_general | solution.py:47
  182.4 4.6 %fusion.109 = bf16[1024,256]{1,0:T(8,128)(2,1)S(1)} fusion(bf16[256,256]{1,0:T(8,128)(2,1)S(1)} %get-tuple-element.518, f32[256]{0:T(256)S(1)} %get-tuple-element.467, f32[256]{0:T(256)S(1)} %get-tuple-element.468, f32[256]{0:T(256)S(1)} %get-tuple-element.469, f32[1024]{0:T(1024)S(1)} %bitcast.98, f32[256]{0:T(256)S(1)} %get-tuple-element.471, ...), kind=kOutput, calls=%fused_computation.12.clone.1 | convolution fusion | flops 137101312 | bytes 672768 | tf_op jit(solution)/shard_map/while/body/eval_jaxpr/dot_general | solution.py:47
  195.5 4.6 %fusion.109 = bf16[1024,256]{1,0:T(8,128)(2,1)S(1)} fusion(bf16[256,256]{1,0:T(8,128)(2,1)S(1)} %get-tuple-element.518, f32[256]{0:T(256)S(1)} %get-tuple-element.467, f32[256]{0:T(256)S(1)} %get-tuple-element.468, f32[256]{0:T(256)S(1)} %get-tuple-element.469, f32[1024]{0:T(1024)S(1)} %bitcast.98, f32[256]{0:T(256)S(1)} %get-tuple-element.471, ...), kind=kOutput, calls=%fused_computation.12.clone.1 | convolution fusion | flops 137101312 | bytes 672768 | tf_op jit(solution)/shard_map/while/body/eval_jaxpr/dot_general | solution.py:47
  208.7 4.6 %fusion.109 = bf16[1024,256]{1,0:T(8,128)(2,1)S(1)} fusion(bf16[256,256]{1,0:T(8,128)(2,1)S(1)} %get-tuple-element.518, f32[256]{0:T(256)S(1)} %get-tuple-element.467, f32[256]{0:T(256)S(1)} %get-tuple-element.468, f32[256]{0:T(256)S(1)} %get-tuple-element.469, f32[1024]{0:T(1024)S(1)} %bitcast.98, f32[256]{0:T(256)S(1)} %get-tuple-element.471, ...), kind=kOutput, calls=%fused_computation.12.clone.1 | convolution fusion | flops 137101312 | bytes 672768 | tf_op jit(solution)/shard_map/while/body/eval_jaxpr/dot_general | solution.py:47
  221.9 4.6 %fusion.109 = bf16[1024,256]{1,0:T(8,128)(2,1)S(1)} fusion(bf16[256,256]{1,0:T(8,128)(2,1)S(1)} %get-tuple-element.518, f32[256]{0:T(256)S(1)} %get-tuple-element.467, f32[256]{0:T(256)S(1)} %get-tuple-element.468, f32[256]{0:T(256)S(1)} %get-tuple-element.469, f32[1024]{0:T(1024)S(1)} %bitcast.98, f32[256]{0:T(256)S(1)} %get-tuple-element.471, ...), kind=kOutput, calls=%fused_computation.12.clone.1 | convolution fusion | flops 137101312 | bytes 672768 | tf_op jit(solution)/shard_map/while/body/eval_jaxpr/dot_general | solution.py:47
  235.1 4.6 %fusion.109 = bf16[1024,256]{1,0:T(8,128)(2,1)S(1)} fusion(bf16[256,256]{1,0:T(8,128)(2,1)S(1)} %get-tuple-element.518, f32[256]{0:T(256)S(1)} %get-tuple-element.467, f32[256]{0:T(256)S(1)} %get-tuple-element.468, f32[256]{0:T(256)S(1)} %get-tuple-element.469, f32[1024]{0:T(1024)S(1)} %bitcast.98, f32[256]{0:T(256)S(1)} %get-tuple-element.471, ...), kind=kOutput, calls=%fused_computation.12.clone.1 | convolution fusion | flops 137101312 | bytes 672768 | tf_op jit(solution)/shard_map/while/body/eval_jaxpr/dot_general | solution.py:47
  248.2 4.6 %fusion.109 = bf16[1024,256]{1,0:T(8,128)(2,1)S(1)} fusion(bf16[256,256]{1,0:T(8,128)(2,1)S(1)} %get-tuple-element.518, f32[256]{0:T(256)S(1)} %get-tuple-element.467, f32[256]{0:T(256)S(1)} %get-tuple-element.468, f32[256]{0:T(256)S(1)} %get-tuple-element.469, f32[1024]{0:T(1024)S(1)} %bitcast.98, f32[256]{0:T(256)S(1)} %get-tuple-element.471, ...), kind=kOutput, calls=%fused_computation.12.clone.1 | convolution fusion | flops 137101312 | bytes 672768 | tf_op jit(solution)/shard_map/while/body/eval_jaxpr/dot_general | solution.py:47
  264.6 38.0 %reduce-scatter.2.cloned.1.call-done = bf16[128,1024]{1,0:T(8,128)(2,1)} async-done(((bf16[1024,1024]{1,0:T(8,128)(2,1)}), bf16[128,1024]{1,0:T(8,128)(2,1)}) %reduce-scatter.2.cloned.1.call-update) | async-done | bytes 262160 | tf_op jit(solution)/shard_map/reduce_scatter | solution.py:188
  303.3 4.6 %all-to-all-start.3 = ((f32[3,32,8]{2,0,1:T(4,128)}), f32[3,32,8]{2,0,1:T(4,128)S(1)}, u32[]{:S(2)}, u32[]{:S(2)}) async-start(f32[3,32,8]{2,0,1:T(4,128)} %copy.39), calls=%async_computation.3 | async-start | bytes 131072 | tf_op jit(solution)/shard_map/all_to_all | solution.py:174
  308.9 15.9 %all-reduce = (f32[]{:T(128)}, f32[1024]{0:T(1024)S(1)}) all-reduce(f32[]{:T(128)} %get-tuple-element.221, f32[1024]{0:T(1024)S(1)} %get-tuple-element.326), channel_id=1, replica_groups=mesh['grp'=4,'shard'=8] {'shard'}, use_global_device_ids=true, to_apply=%region_15.16 | all-reduce | flops 1025 | bytes 8200 | tf_op jit(solution)/shard_map/psum | solution.py:12
  324.8 12.4 %all-reduce.1 = (f32[]{:T(128)}, f32[1024]{0:T(1024)}) all-reduce(f32[]{:T(128)} %get-tuple-element.355, f32[1024]{0:T(1024)S(1)} %get-tuple-element.356), channel_id=1, replica_groups=mesh['grp'=4,'shard'=8] {'grp'}, use_global_device_ids=true, to_apply=%region_16.17 | all-reduce | flops 1025 | bytes 8200 | tf_op jit(solution)/shard_map/psum | solution.py:12
  (613 shorter events, 124.9 us)
Async XLA Ops:
  7.2 33.9 %copy-start.1 = (bf16[128,1024]{1,0:T(8,128)(2,1)S(1)}, bf16[128,1024]{1,0:T(8,128)(2,1)}, u32[]{:S(2)}) copy-start(bf16[128,1024]{1,0:T(8,128)(2,1)} %param.10) | copy-start | bytes 786436
  7.2 33.9 %copy-start.2 = (f32[1024]{0:T(1024)S(1)}, f32[1024]{0:T(1024)}, u32[]{:S(2)}) copy-start(f32[1024]{0:T(1024)} %param.12) | copy-start | bytes 12292
  7.2 33.9 %all-gather.2.cloned.1.call-start = ((), (), s32[]{:S(2)}) async-start(), calls=%async_computation.5 | async-start | bytes 2359296 | tf_op jit(solution)/shard_map/all_gather | solution.py:119
  10.9 14.5 %all-to-all-start.1 = ((f32[32,8,1]{1,2,0:T(1,128)}), f32[32,8,1]{1,2,0:T(1,128)S(1)}, u32[]{:S(2)}, u32[]{:S(2)}) async-start(f32[32,8,1]{1,2,0:T(1,128)} %bitcast.2), calls=%async_computation.1 | async-start | bytes 32768 | tf_op jit(solution)/shard_map/all_to_all | solution.py:139
  25.4 11.6 %all-to-all-start.2 = ((f32[32,8,3]{1,2,0:T(4,128)}), f32[32,8,3]{1,2,0:T(4,128)S(1)}, u32[]{:S(2)}, u32[]{:S(2)}) async-start(f32[32,8,3]{1,2,0:T(4,128)} %copy.35), calls=%async_computation.2 | async-start | bytes 131072 | tf_op jit(solution)/shard_map/all_to_all | solution.py:138
  37.0 13.3 %copy-start.3 = (bf16[4,256]{1,0:T(4,128)(2,1)S(1)}, bf16[4,256]{1,0:T(4,128)(2,1)}, u32[]{:S(2)}) copy-start(bf16[4,256]{1,0:T(4,128)(2,1)} %param.13) | copy-start | bytes 6148
  37.0 13.3 %all-to-all-start = ((f32[32,8,256]{2,1,0:T(8,128)}), f32[32,8,256]{2,1,0:T(8,128)S(1)}, u32[]{:S(2)}, u32[]{:S(2)}) async-start(f32[32,8,256]{2,1,0:T(8,128)} %bitcast), calls=%async_computation | async-start | bytes 524288 | tf_op jit(solution)/shard_map/all_to_all | solution.py:137
  39.7 262.8 %reduce-scatter.2.cloned.1.call-start = ((), (), s32[]{:S(2)}) async-start(), calls=%async_computation.6 | async-start | bytes 2359296 | tf_op jit(solution)/shard_map/reduce_scatter | solution.py:188
  261.4 2.2 copy-start
  263.6 76.8 %all-reduce.4.cloned.1.call-start = ((), (), s32[]{:S(2)}) async-start(), calls=%async_computation.7 | async-start | bytes 524288 | tf_op jit(solution)/shard_map/psum | solution.py:196
  303.3 33.9 %all-to-all-start.3 = ((f32[3,32,8]{2,0,1:T(4,128)}), f32[3,32,8]{2,0,1:T(4,128)S(1)}, u32[]{:S(2)}, u32[]{:S(2)}) async-start(f32[3,32,8]{2,0,1:T(4,128)} %copy.39), calls=%async_computation.3 | async-start | bytes 131072 | tf_op jit(solution)/shard_map/all_to_all | solution.py:174
Sparse Core Ops, SparseCore 0:
  9.9 31.1 all-gather.1
  263.7 38.8 reduce-scatter.1
  304.9 35.4 all-reduce.3
